TPU v7x, 32 devices: a whole 2x2x4 slice. The times are simulated.
32 devices in a mesh: fields: 2 (over x), prow: 8 (over z, y), pcol: 2 (over core).
Axes of the slice: x: 2, y: 2, z: 4, core: 2. Of those that a mesh axis runs over, the one named last changes fastest.
Arguments:
- inverse_tiles: bfloat16 [32, 16, 256, 256], P(('fields', 'prow'), 'pcol'), parts along dimension 0, may hold values from -6 to 6
- panel_blocks: bfloat16 [4, 8, 256, 512], P('fields', 'prow', None, 'pcol'), parts along dimension 0, may hold values from -0.125 to 0.125
- diag_inverse: float32 [4, 512], P('fields', 'pcol'), parts along dimension 0, may hold values from 0.5 to 2
- structure: int32 [4, 8], P('fields'), parts along dimension 0, may hold values from 0 to 15, as said below
- block_slot: int32 [32], P('fields'), parts along dimension 0, may hold values from 0 to 15, each once
Outputs:
- sigma_new: bfloat16 [4, 16, 256, 512], P('fields', 'prow', None, 'pcol'), parts along dimension 0
- variances: float32 [4, 512], P('fields', 'pcol'), parts along dimension 0
There are 2 independent parts, one for each index of `fields`. A program takes and returns all parts, laid end to end along the dimension named above; each array names one. Nothing has to cross between parts.
Inputs may be any that keep to these rules, and one draw needn't show every extreme that they name: `structure`: each row lists 8 distinct row blocks in increasing order, and the last is always 16 - 1. `block_slot`: each slot is used by exactly one row block.
All inputs are finite; a program needn't handle non-finite values.
Results may differ from a plain program's by a relative error of at most 0.0006.
Values may be sent and summed in bfloat16 or wider, within the bound.
No kernel may reach another device: no remote copies, remote signals or barrier semaphores. Data moves between devices by JAX's collectives and lax.ppermute only.
A program may use at most 128 MiB of HBM per device.

v0:
```python
import jax
import jax.numpy as jnp
from jax import lax
from jax.sharding import PartitionSpec as P


def swapped(shard, axis, stride):
    return lax.ppermute(shard, axis, [(i, i ^ 1 << stride) for i in range(lax.axis_size(axis))])


def make_accumulate(selected, row_hits, piece):
    contrib = jnp.einsum("iskxy,skyw->sixw", selected, piece, preferred_element_type=jnp.float32)
    own_panel = jnp.einsum("sik,skxw->sixw", row_hits, piece, preferred_element_type=jnp.float32)
    return (contrib, own_panel)


def per_device(inverse_tiles, panel_blocks, diag_inverse, structure, block_slot):
    rows_here = inverse_tiles.shape[0]
    tile_size = inverse_tiles.shape[2]
    supernodes = panel_blocks.shape[0]
    positions = structure.shape[1]
    prow_index = lax.axis_index("prow")
    pcol_index = lax.axis_index("pcol")
    slot_of = block_slot[structure]
    own_rows = prow_index * rows_here + jnp.arange(rows_here, dtype=jnp.int32)
    row_match = slot_of[:, None, :] == own_rows[None, :, None]
    row_hits = row_match.astype(jnp.bfloat16)
    row_used = jnp.any(row_match, axis=2)
    partner = swapped(inverse_tiles, "pcol", 0)
    first_half = jnp.where(pcol_index == 0, inverse_tiles, partner)
    second_half = jnp.where(pcol_index == 0, partner, inverse_tiles)
    whole_rows = jnp.concatenate([first_half, second_half], axis=1)
    selected = jnp.take(whole_rows, slot_of.reshape(-1), axis=1)
    selected = selected.reshape(rows_here, supernodes, positions, tile_size, tile_size)
    summed, own_panel = make_accumulate(
        selected, row_hits, lax.all_gather(panel_blocks, "prow", axis=1, tiled=True)
    )
    sigma_rows = jnp.where(row_used[:, :, None, None], -summed, jnp.zeros((), jnp.float32))
    partial_value = jnp.sum(own_panel * sigma_rows, axis=(1, 2))
    correction = lax.psum(partial_value, "prow")
    variances = diag_inverse - correction
    return (sigma_rows.astype(jnp.bfloat16), variances)


def solution(mesh):
    in_specs = (
        P(("fields", "prow"), "pcol", None, None),
        P("fields", "prow", None, "pcol"),
        P("fields", "pcol"),
        P("fields", None),
        P("fields"),
    )
    out_specs = (P("fields", "prow", None, "pcol"), P("fields", "pcol"))
    return jax.shard_map(
        per_device, mesh=mesh, in_specs=in_specs, out_specs=out_specs, check_vma=False
    )
```

profile of v0, /device:TPU:0, one launch (start us, length us, event | category | flops | bytes accessed | tf_op | source)
XLA Modules:
  0.0 95.9 jit_solution(17099047433927221169)
XLA Ops:
  7.2 0.0 copy-start
  7.2 0.0 all-gather.2.cloned.1.call-start
  7.2 0.7 all-gather.2.cloned.1.call-update
  7.9 0.6 collective-permute-start
  8.5 0.7 compare_select_fusion.1
  9.2 0.1 reshape.53
  9.2 0.0 copy-done
  9.2 0.7 gather_fusion
  9.9 0.1 reshape.52
  10.0 0.2 compare_reduce_fusion
  10.2 2.3 %collective-permute-done = bf16[2,8,256,256]{3,2,1,0:T(8,128)(2,1)S(1)} collective-permute-done((bf16[2,8,256,256]{3,2,1,0:T(8,128)(2,1)}, bf16[2,8,256,256]{3,2,1,0:T(8,128)(2,1)S(1)}, u32[]{:S(2)}, u32[]{:S(2)}) %collective-permute-start) | collective-permute-done | bytes 2097184 | tf_op jit(solution)/shard_map/ppermute | solution.py:8
  12.5 1.9 %broadcast_select_fusion.1 = (bf16[2,8,256,256]{3,2,1,0:T(8,128)(2,1)S(1)}, bf16[2,8,256,256]{3,2,1,0:T(8,128)(2,1)S(1)}) fusion(bf16[2,8,256,256]{3,2,1,0:T(8,128)(2,1)} %param.5, bf16[2,8,256,256]{3,2,1,0:T(8,128)(2,1)S(1)} %collective-permute-done, pred[]{:T(512)S(6)} %eq.20), kind=kLoop, calls=%fused_computation.11 | loop fusion | flops 2097152 | bytes 8388609 | tf_op jit(solution)/shard_map/jit(_where)/select_n | solution.py:30
  14.3 2.3 %pad_maximum_fusion = bf16[2,16,256,256]{3,2,1,0:T(8,128)(2,1)} fusion(bf16[2,8,256,256]{3,2,1,0:T(8,128)(2,1)S(1)} %get-tuple-element.3, bf16[2,8,256,256]{3,2,1,0:T(8,128)(2,1)S(1)} %get-tuple-element.2), kind=kLoop, calls=%fused_computation.2 | loop fusion | flops 2097152 | bytes 8388608 | tf_op jit(solution)/shard_map/concatenate | solution.py:32
  16.7 4.9 %gather_fusion.1 = bf16[16,2,256,256]{3,2,1,0:T(8,128)(2,1)} fusion(bf16[2,16,256,256]{3,2,1,0:T(8,128)(2,1)} %pad_maximum_fusion, s32[1024]{0:T(1024)S(1)} %pad_clamp_fusion), kind=kCustom, calls=%fused_computation.1 | custom fusion | bytes 8388672 | tf_op jit(solution)/shard_map/jit(_take)/gather | solution.py:33
  21.6 40.4 %all-gather.2.cloned.1.call-done = bf16[2,8,256,256]{3,2,1,0:T(8,128)(2,1)} async-done(((bf16[2,1,256,256]{3,2,1,0:T(8,128)(2,1)}), bf16[2,8,256,256]{3,2,1,0:T(8,128)(2,1)}) %all-gather.2.cloned.1.call-update) | async-done | bytes 2097168 | tf_op jit(solution)/shard_map/all_gather | solution.py:36
  62.0 0.0 copy-start.1
  62.0 3.2 %fusion.3 = f32[2,2,256,256]{3,1,2,0:T(2,128)S(1)} fusion(bf16[2,8,256,256]{3,2,1,0:T(8,128)(2,1)} %all-gather.2.cloned.1.call-done, s32[2,8]{1,0:T(2,128)S(1)} %reshape.52, s32[2]{0:T(128)S(1)} %iota_add_fusion), kind=kOutput, calls=%fused_computation.7 | convolution fusion | flops 4194336 | bytes 3145800 | tf_op jit(solution)/shard_map/sik,skxw->sixw/dot_general | solution.py:13
  65.2 0.0 copy-done.1
  65.2 0.0 copy-start.2
  65.2 4.3 %fusion.15 = (f32[2,256]{1,0:T(2,128)S(1)}, bf16[2,2,256,256]{3,2,1,0:T(8,128)(2,1)}) fusion(f32[2,2,256,256]{3,1,2,0:T(2,128)S(1)} %fusion.3, bf16[2,8,256,256]{3,2,1,0:T(8,128)(2,1)S(1)} %copy-done.1, bf16[2,2,8,256,256]{4,3,0,2,1:T(8,128)(2,1)} %bitcast.32, pred[2,8]{1,0:T(4,128)(4,1)S(1)} %compare_and_fusion, pred[2,2]{1,0:T(4,128)(4,1)S(1)} %compare_reduce_fusion), kind=kOutput, calls=%fused_computation.16 | convolution fusion | flops 1077149184 | bytes 7866388 | tf_op jit(solution)/shard_map/iskxy,skyw->sixw/dot_general | solution.py:12
  69.5 19.0 %psum.7 = f32[2,256]{1,0:T(2,128)S(1)} all-reduce(f32[2,256]{1,0:T(2,128)S(1)} %get-tuple-element.4), channel_id=1, replica_groups=mesh['fields'=2,'prow'=8,'pcol'=2] {'prow'}, use_global_device_ids=true, to_apply=%region_2.3 | all-reduce | flops 512 | bytes 4096 | tf_op jit(solution)/shard_map/psum | solution.py:40
  88.5 0.0 copy-done.2
  88.5 0.6 sub.3
  (5 shorter events, 0.0 us)
Async XLA Ops:
  7.2 2.1 %copy-start = (s32[16]{0:T(128)S(1)}, s32[16]{0:T(128)}, u32[]{:S(2)}) copy-start(s32[16]{0:T(128)} %param.9) | copy-start | bytes 196
  7.2 54.8 %all-gather.2.cloned.1.call-start = ((), (), s32[]{:S(2)}) async-start(), calls=%async_computation | async-start | bytes 2359296 | tf_op jit(solution)/shard_map/all_gather | solution.py:36
  7.9 4.6 %collective-permute-start = (bf16[2,8,256,256]{3,2,1,0:T(8,128)(2,1)}, bf16[2,8,256,256]{3,2,1,0:T(8,128)(2,1)S(1)}, u32[]{:S(2)}, u32[]{:S(2)}) collective-permute-start(bf16[2,8,256,256]{3,2,1,0:T(8,128)(2,1)} %param.5), channel_id=1, source_target_pairs={{0,1},{1,0},{2,3},{3,2},{4,5},{5,4},{6,7},{7,6},{8,9},{9,8},{10,11... | collective-permute-start | bytes 6291464 | tf_op jit(solution)/shard_map/ppermute | solution.py:8
  62.0 3.2 %copy-start.1 = (bf16[2,8,256,256]{3,2,1,0:T(8,128)(2,1)S(1)}, bf16[2,8,256,256]{3,2,1,0:T(8,128)(2,1)}, u32[]{:S(2)}) copy-start(bf16[2,8,256,256]{3,2,1,0:T(8,128)(2,1)} %all-gather.2.cloned.1.call-done) | copy-start | bytes 6291460
  65.2 23.3 %copy-start.2 = (f32[2,256]{1,0:T(2,128)S(1)}, f32[2,256]{1,0:T(2,128)}, u32[]{:S(2)}) copy-start(f32[2,256]{1,0:T(2,128)} %param.7) | copy-start | bytes 6148
Sparse Core Ops, SparseCore 0:
  10.2 51.7 all-gather.1
where the time goes:
time: 96.1 us; the launch traced here: 95.9 us
  waiting for transfers between devices  43.3 us (45%)
  blocking collectives  19 us (20%)
  between operations  14.1 us (15%)
  matrix products  7.51 us (8%)
  local copies, waits for them, and re-layouts  5.78 us (6%)
  other arithmetic  5.67 us (6%)
    all_gather x1, waiting for transfers between devices, per_device(): lax.all_gather(panel_blocks, 'prow', axis=1, tiled=True)  40.4 us
    psum x1, blocking collectives, per_device(): correction = lax.psum(partial_value, 'prow')  19 us
    gather x1, local copies, waits for them, and re-layouts, per_device(): selected = jnp.take(whole_rows, slot_of.reshape(-1), axis=1)  4.94 us
    dot_general x1, matrix products, make_accumulate(): jnp.einsum('iskxy,skyw->sixw', selected, piece, preferred_element_type=jn...  4.32 us
    dot_general x1, matrix products, make_accumulate(): jnp.einsum('sik,skxw->sixw', row_hits, piece, preferred_element_type=jnp....  3.19 us
    concatenate x1, other arithmetic, per_device(): whole_rows = jnp.concatenate([first_half, second_half], axis=1)  2.33 us
    ppermute x1, waiting for transfers between devices, swapped(): lax.ppermute(shard, axis, [(i, i ^ 1 << stride) for i in range(lax.axis_s...  2.26 us
  transfers between devices with their start and end apart: 2, of which 2 were waited for; matrix products, arithmetic and copies ran while one was open for 11% of the time, Pallas kernels for 0%

commit v1 on v0

--- a/solution.py
+++ b/solution.py
@@ -2,6 +2,27 @@
 import jax.numpy as jnp
 from jax import lax
 from jax.sharding import PartitionSpec as P
+
+
+def open_widths_by_axis(obj, axis_no):
+    obj = jnp.moveaxis(obj, 0, axis_no)
+    clean = obj.shape
+    new = obj.reshape(*clean[:axis_no], clean[axis_no] * clean[axis_no + 1], *clean[axis_no + 2 :])
+    return new
+
+
+def scan_edges(arr, device_axis):
+    count_all = jax.lax.axis_size(device_axis)
+    later = arr[None]
+    for hop_no in range(count_all.bit_length() - 1):
+        value_now = 1 << hop_no
+        low = jax.lax.ppermute(
+            later, axis_name=device_axis, perm=[(h, h ^ value_now) for h in range(count_all)]
+        )
+        step_out = jnp.stack([later, low])
+        everything = jax.lax.axis_index(device_axis) >> hop_no & 1
+        later = jnp.where(everything == 0, step_out, step_out[::-1]).reshape(-1, *arr.shape)
+    return later
 
 
 def swapped(shard, axis, stride):
@@ -32,9 +53,12 @@
     whole_rows = jnp.concatenate([first_half, second_half], axis=1)
     selected = jnp.take(whole_rows, slot_of.reshape(-1), axis=1)
     selected = selected.reshape(rows_here, supernodes, positions, tile_size, tile_size)
-    summed, own_panel = make_accumulate(
-        selected, row_hits, lax.all_gather(panel_blocks, "prow", axis=1, tiled=True)
-    )
+
+    def order_the_row(array_here, content, in_dim):
+        local_out = open_widths_by_axis(scan_edges(array_here, content), in_dim)
+        return local_out
+
+    summed, own_panel = make_accumulate(selected, row_hits, order_the_row(panel_blocks, "prow", 1))
     sigma_rows = jnp.where(row_used[:, :, None, None], -summed, jnp.zeros((), jnp.float32))
     partial_value = jnp.sum(own_panel * sigma_rows, axis=(1, 2))
     correction = lax.psum(partial_value, "prow")

time: 96.1 us -> 110 us (1.14)
  waiting for transfers between devices: 43.3 us -> 61.1 us
  between operations: 14.1 us -> 0.69 us
  starting transfers between devices: 0.6 us -> 7.52 us
  blocking collectives: 19 us -> 21.2 us
  other arithmetic: 5.67 us -> 7.71 us
  matrix products: 7.51 us -> 5.76 us
    ppermute x0 -> x3, waiting for transfers between devices: none -> 61 us  [scan_edges(): jax.lax.ppermute(later, axis_name=device_axis, perm=[(h, h ^ value_now) f...]
    all_gather x1 -> x0, waiting for transfers between devices: 40.4 us -> none  [per_device(): lax.all_gather(panel_blocks, 'prow', axis=1, tiled=True)]
    ppermute x0 -> x3, starting transfers between devices: none -> 7.52 us  [scan_edges(): jax.lax.ppermute(later, axis_name=device_axis, perm=[(h, h ^ value_now) f...]
    ppermute x1, waiting for transfers between devices: 2.26 us -> 0.01 us  [swapped(): lax.ppermute(shard, axis, [(i, i ^ 1 << stride) for i in range(lax.axis_s...]
    psum x1, blocking collectives: 19 us -> 21.2 us  [per_device(): correction = lax.psum(partial_value, 'prow')]
    dot_general x1, matrix products: 3.19 us -> 1.45 us  [make_accumulate(): jnp.einsum('sik,skxw->sixw', row_hits, piece, preferred_element_type=jnp....]
    another operation x0 -> x4, other arithmetic: none -> 1.41 us  [scan_edges(): step_out = jnp.stack([later, low])]
  transfers between devices with their start and end apart: 2 -> 4, of which waited for: 2 -> 3; matrix products, arithmetic and copies ran while one was open for 11% -> 3% of each run, Pallas kernels for 0% -> 0%
where the time goes in v1:
time: 110 us
  waiting for transfers between devices  61.1 us (56%)
  blocking collectives  21.2 us (19%)
  other arithmetic  7.71 us (7%)
  starting transfers between devices  7.52 us (7%)
  local copies, waits for them, and re-layouts  5.8 us (5%)
  matrix products  5.76 us (5%)
    ppermute x3, waiting for transfers between devices, scan_edges(): jax.lax.ppermute(later, axis_name=device_axis, perm=[(h, h ^ value_now) f...  61 us
    psum x1, blocking collectives, per_device(): correction = lax.psum(partial_value, 'prow')  21.2 us
    ppermute x3, starting transfers between devices, scan_edges(): jax.lax.ppermute(later, axis_name=device_axis, perm=[(h, h ^ value_now) f...  7.52 us
    gather x1, local copies, waits for them, and re-layouts, per_device(): selected = jnp.take(whole_rows, slot_of.reshape(-1), axis=1)  4.96 us
    dot_general x1, matrix products, make_accumulate(): jnp.einsum('iskxy,skyw->sixw', selected, piece, preferred_element_type=jn...  4.31 us
    select_n x1, other arithmetic, per_device(): first_half = jnp.where(pcol_index == 0, inverse_tiles, partner)  2.5 us
    concatenate x1, other arithmetic, per_device(): whole_rows = jnp.concatenate([first_half, second_half], axis=1)  2.3 us
  transfers between devices with their start and end apart: 4, of which 3 were waited for; matrix products, arithmetic and copies ran while one was open for 3% of the time, Pallas kernels for 0%

profile of v1, /device:TPU:0, one launch (start us, length us, event | category | flops | bytes accessed | tf_op | source)
XLA Modules:
  0.0 109.7 jit_solution(16270197471320280172)
XLA Ops:
  0.6 0.0 copy-start
  0.6 3.1 %collective-permute-start.1 = (bf16[1,2,1,256,256]{4,3,1,2,0:T(8,128)(2,1)}, bf16[1,2,1,256,256]{4,3,1,2,0:T(8,128)(2,1)S(1)}, u32[]{:S(2)}, u32[]{:S(2)}) collective-permute-start(bf16[1,2,1,256,256]{4,3,1,2,0:T(8,128)(2,1)} %bitcast.47), channel_id=1, source_target_pairs={{0,2},{2,0},{4,6},{6,4},{8,10},{10,8},{12,14},{14,12},{1,3},{3,1},... | collective-permute-start | bytes 786440 | tf_op jit(solution)/shard_map/ppermute | solution.py:19
  3.7 6.5 %collective-permute-done.1 = bf16[1,2,1,256,256]{4,3,1,2,0:T(8,128)(2,1)S(1)} collective-permute-done((bf16[1,2,1,256,256]{4,3,1,2,0:T(8,128)(2,1)}, bf16[1,2,1,256,256]{4,3,1,2,0:T(8,128)(2,1)S(1)}, u32[]{:S(2)}, u32[]{:S(2)}) %collective-permute-start.1) | collective-permute-done | bytes 262176 | tf_op jit(solution)/shard_map/ppermute | solution.py:19
  10.2 1.0 pad_maximum_fusion.3
  11.2 0.1 fusion.18
  11.4 1.9 %collective-permute-start.2 = (bf16[2,2,1,256,256]{4,3,1,0,2:T(8,128)(2,1)S(1)}, bf16[2,2,1,256,256]{4,3,1,0,2:T(8,128)(2,1)S(1)}, u32[]{:S(2)}, u32[]{:S(2)}) collective-permute-start(bf16[2,2,1,256,256]{4,3,1,0,2:T(8,128)(2,1)S(1)} %get-tuple-element.7), channel_id=1, source_target_pairs={{0,4},{2,6},{4,0},{6,2},{8,12},{10,14},{12,8},{14,10},{1,5},{3,7},... | collective-permute-start | bytes 1572872 | tf_op jit(solution)/shard_map/ppermute | solution.py:19
  13.2 0.0 collective-permute-start
  13.2 11.3 %collective-permute-done.2 = bf16[2,2,1,256,256]{4,3,1,0,2:T(8,128)(2,1)S(1)} collective-permute-done((bf16[2,2,1,256,256]{4,3,1,0,2:T(8,128)(2,1)S(1)}, bf16[2,2,1,256,256]{4,3,1,0,2:T(8,128)(2,1)S(1)}, u32[]{:S(2)}, u32[]{:S(2)}) %collective-permute-start.2) | collective-permute-done | bytes 524320 | tf_op jit(solution)/shard_map/ppermute | solution.py:19
  24.5 0.0 copy-start.2
  24.5 0.1 pad_maximum_fusion.2
  24.6 0.2 reverse_select_fusion.1
  24.8 2.6 %collective-permute-start.3 = (bf16[4,2,1,256,256]{4,3,1,0,2:T(8,128)(2,1)S(1)}, bf16[4,2,1,256,256]{4,3,1,0,2:T(8,128)(2,1)S(1)}, u32[]{:S(2)}, u32[]{:S(2)}) collective-permute-start(bf16[4,2,1,256,256]{4,3,1,0,2:T(8,128)(2,1)S(1)} %bitcast.43), channel_id=1, source_target_pairs={{0,8},{2,10},{4,12},{6,14},{8,0},{10,2},{12,4},{14,6},{1,9},{3,11}... | collective-permute-start | bytes 3145736 | tf_op jit(solution)/shard_map/ppermute | solution.py:19
  27.4 0.0 copy-done.2
  27.4 0.1 reshape.69
  27.5 0.0 copy-done
  27.5 0.7 gather_fusion
  28.2 0.1 reshape.68
  28.3 0.2 compare_reduce_fusion
  28.5 43.2 %collective-permute-done.3 = bf16[4,2,1,256,256]{4,3,1,0,2:T(8,128)(2,1)S(1)} collective-permute-done((bf16[4,2,1,256,256]{4,3,1,0,2:T(8,128)(2,1)S(1)}, bf16[4,2,1,256,256]{4,3,1,0,2:T(8,128)(2,1)S(1)}, u32[]{:S(2)}, u32[]{:S(2)}) %collective-permute-start.3) | collective-permute-done | bytes 1048608 | tf_op jit(solution)/shard_map/ppermute | solution.py:19
  71.7 0.2 pad_maximum_fusion.1
  71.9 0.5 reverse_select_fusion
  72.4 1.4 %fusion.2 = f32[2,2,256,256]{3,1,2,0:T(2,128)S(1)} fusion(bf16[8,2,1,256,256]{4,3,1,0,2:T(8,128)(2,1)S(1)} %bitcast.40, s32[2,8]{1,0:T(2,128)S(1)} %reshape.68, s32[2]{0:T(128)S(1)} %iota_add_fusion), kind=kOutput, calls=%fused_computation.8 | convolution fusion | flops 4194336 | bytes 3145800 | tf_op jit(solution)/shard_map/sik,skxw->sixw/dot_general | solution.py:34
  73.9 0.0 collective-permute-done
  73.9 2.5 %broadcast_select_fusion.1 = (bf16[2,8,256,256]{3,2,1,0:T(8,128)(2,1)S(1)}, bf16[2,8,256,256]{3,2,1,0:T(8,128)(2,1)S(1)}) fusion(bf16[2,8,256,256]{3,2,1,0:T(8,128)(2,1)} %param.5, bf16[2,8,256,256]{3,2,1,0:T(8,128)(2,1)} %collective-permute-done, pred[]{:T(512)S(6)} %eq.29), kind=kLoop, calls=%fused_computation.14 | loop fusion | flops 2097152 | bytes 8388609 | tf_op jit(solution)/shard_map/jit(_where)/select_n | solution.py:51
  76.4 2.3 %pad_maximum_fusion = bf16[2,16,256,256]{3,2,1,0:T(8,128)(2,1)} fusion(bf16[2,8,256,256]{3,2,1,0:T(8,128)(2,1)S(1)} %get-tuple-element.3, bf16[2,8,256,256]{3,2,1,0:T(8,128)(2,1)S(1)} %get-tuple-element.2), kind=kLoop, calls=%fused_computation.2 | loop fusion | flops 2097152 | bytes 8388608 | tf_op jit(solution)/shard_map/concatenate | solution.py:53
  78.7 5.0 %gather_fusion.1 = bf16[16,2,256,256]{3,2,1,0:T(8,128)(2,1)} fusion(bf16[2,16,256,256]{3,2,1,0:T(8,128)(2,1)} %pad_maximum_fusion, s32[1024]{0:T(1024)S(1)} %pad_clamp_fusion), kind=kCustom, calls=%fused_computation.1 | custom fusion | bytes 8388672 | tf_op jit(solution)/shard_map/jit(_take)/gather | solution.py:54
  83.6 0.0 copy-start.1
  83.6 4.3 %fusion.16 = (f32[2,256]{1,0:T(2,128)S(1)}, bf16[2,2,256,256]{3,2,1,0:T(8,128)(2,1)}) fusion(f32[2,2,256,256]{3,1,2,0:T(2,128)S(1)} %fusion.2, bf16[2,8,256,256,1]{3,2,0,1,4:T(8,128)(2,1)S(1)} %bitcast.41, bf16[2,2,8,256,256]{4,3,0,2,1:T(8,128)(2,1)} %bitcast.42, pred[2,8]{1,0:T(4,128)(4,1)S(1)} %compare_and_fusion, pred[2,2]{1,0:T(4,128)(4,1)S(1)} %compare_reduce_fusion), kind=kOutput, calls=%fused_computation.21 | convolution fusion | flops 1077149184 | bytes 7866388 | tf_op jit(solution)/shard_map/iskxy,skyw->sixw/dot_general | solution.py:33
  88.0 21.2 %psum.7 = f32[2,256]{1,0:T(2,128)S(1)} all-reduce(f32[2,256]{1,0:T(2,128)S(1)} %get-tuple-element.4), channel_id=1, replica_groups=mesh['fields'=2,'prow'=8,'pcol'=2] {'prow'}, use_global_device_ids=true, to_apply=%region_2.3 | all-reduce | flops 512 | bytes 4096 | tf_op jit(solution)/shard_map/psum | solution.py:64
  109.2 0.0 copy-done.1
  109.2 0.6 sub.3
  (6 shorter events, 0.0 us)
Async XLA Ops:
  0.6 26.9 %copy-start = (s32[16]{0:T(128)S(1)}, s32[16]{0:T(128)}, u32[]{:S(2)}) copy-start(s32[16]{0:T(128)} %param.9) | copy-start | bytes 196
  0.6 9.6 %collective-permute-start.1 = (bf16[1,2,1,256,256]{4,3,1,2,0:T(8,128)(2,1)}, bf16[1,2,1,256,256]{4,3,1,2,0:T(8,128)(2,1)S(1)}, u32[]{:S(2)}, u32[]{:S(2)}) collective-permute-start(bf16[1,2,1,256,256]{4,3,1,2,0:T(8,128)(2,1)} %bitcast.47), channel_id=1, source_target_pairs={{0,2},{2,0},{4,6},{6,4},{8,10},{10,8},{12,14},{14,12},{1,3},{3,1},... | collective-permute-start | bytes 786440 | tf_op jit(solution)/shard_map/ppermute | solution.py:19
  11.4 13.2 %collective-permute-start.2 = (bf16[2,2,1,256,256]{4,3,1,0,2:T(8,128)(2,1)S(1)}, bf16[2,2,1,256,256]{4,3,1,0,2:T(8,128)(2,1)S(1)}, u32[]{:S(2)}, u32[]{:S(2)}) collective-permute-start(bf16[2,2,1,256,256]{4,3,1,0,2:T(8,128)(2,1)S(1)} %get-tuple-element.7), channel_id=1, source_target_pairs={{0,4},{2,6},{4,0},{6,2},{8,12},{10,14},{12,8},{14,10},{1,5},{3,7},... | collective-permute-start | bytes 1572872 | tf_op jit(solution)/shard_map/ppermute | solution.py:19
  13.2 60.7 %collective-permute-start = (bf16[2,8,256,256]{3,2,1,0:T(8,128)(2,1)}, bf16[2,8,256,256]{3,2,1,0:T(8,128)(2,1)}, u32[]{:S(2)}, u32[]{:S(2)}) collective-permute-start(bf16[2,8,256,256]{3,2,1,0:T(8,128)(2,1)} %param.5), channel_id=1, source_target_pairs={{0,1},{1,0},{2,3},{3,2},{4,5},{5,4},{6,7},{7,6},{8,9},{9,8},{10,11... | collective-permute-start | bytes 6291464 | tf_op jit(solution)/shard_map/ppermute | solution.py:29
  24.5 2.9 %copy-start.2 = (s32[2,8]{1,0:T(2,128)S(1)}, s32[2,8]{1,0:T(2,128)}, u32[]{:S(2)}) copy-start(s32[2,8]{1,0:T(2,128)} %param.8) | copy-start | bytes 196
  24.8 46.9 %collective-permute-start.3 = (bf16[4,2,1,256,256]{4,3,1,0,2:T(8,128)(2,1)S(1)}, bf16[4,2,1,256,256]{4,3,1,0,2:T(8,128)(2,1)S(1)}, u32[]{:S(2)}, u32[]{:S(2)}) collective-permute-start(bf16[4,2,1,256,256]{4,3,1,0,2:T(8,128)(2,1)S(1)} %bitcast.43), channel_id=1, source_target_pairs={{0,8},{2,10},{4,12},{6,14},{8,0},{10,2},{12,4},{14,6},{1,9},{3,11}... | collective-permute-start | bytes 3145736 | tf_op jit(solution)/shard_map/ppermute | solution.py:19
  83.6 25.5 %copy-start.1 = (f32[2,256]{1,0:T(2,128)S(1)}, f32[2,256]{1,0:T(2,128)}, u32[]{:S(2)}) copy-start(f32[2,256]{1,0:T(2,128)} %param.7) | copy-start | bytes 6148
